TPU v7x, 256 devices: a whole 4x4x8 slice. The times are simulated.
256 devices in a mesh: cfg: 32 (over y, x, core), tm: 8 (over z).
Axes of the slice: x: 4, y: 4, z: 8, core: 2. Of those that a mesh axis runs over, the one named last changes fastest.
Arguments:
- targets: float32 [8192, 1024], P('cfg', 'tm'), may hold values from -6 to 6
- features: float32 [8192, 64], P('cfg'), may hold values from -6 to 6
- inv_scales: float32 [64], replicated, may hold values from 0.05 to 0.3
- noise: float32 [8192], P('cfg'), may hold values from 0.1 to 1
- time_kernel: float32 [1024, 1024], P('tm'), may hold values from -1 to 1, as said below
- block_mask: int32 [8192, 8], P('cfg', 'tm'), may hold values from 0 to 1, as said below
Outputs:
- solution_field: float32 [8192, 1024], P('cfg', 'tm')
- residual: float32 [8192, 1024], P('cfg', 'tm')
Inputs may be any that keep to these rules, and one draw needn't show every extreme that they name: `block_mask`: each configuration observes one contiguous run of blocks that starts at a block of 0 to 2 and has at least one block; some runs start late and some reach the last block. `time_kernel`: symmetric positive definite, with unit diagonal.
All inputs are finite; a program needn't handle non-finite values.
Results may differ from a plain program's by a relative error of at most 0.00026.
Values sent between devices are 32-bit elements; how exact they have to be, the bound alone decides.
A program may use at most 64 MiB of HBM per device.

v0:
```python
import jax
import jax.numpy as jnp
from jax import lax
from jax.sharding import PartitionSpec as P

BLOCK = 128
ITERS = 2


def matern(left, right):
    cross = jnp.dot(
        left, right.T, precision=lax.Precision.HIGHEST, preferred_element_type=jnp.float32
    )
    dist2 = (
        jnp.sum(left * left, axis=1)[:, None]
        + jnp.sum(right * right, axis=1)[None, :]
        - 2.0 * cross
    )
    scaled_dist = jnp.sqrt(3.0) * jnp.sqrt(jnp.maximum(dist2, 0.0))
    return (1.0 + scaled_dist) * jnp.exp(-scaled_dist)


def body(targets, features, inv_scales, noise, time_kernel, block_mask):
    mask = jnp.repeat(block_mask.astype(jnp.float32), BLOCK, axis=1)
    scaled = features * inv_scales[None, :]
    every = lax.all_gather(scaled, "cfg", axis=0, tiled=True)
    tile = matern(scaled, every)
    residual = mask * targets
    direction = residual
    solution_field = jnp.zeros_like(residual)
    norm_now = lax.psum(jnp.sum(residual * residual), ("cfg", "tm"))
    for step in range(ITERS):
        operate_mixed = jnp.dot(
            tile,
            lax.all_gather(mask * direction, "cfg", axis=0, tiled=True),
            precision=lax.Precision.HIGHEST,
            preferred_element_type=jnp.float32,
        )
        image = (
            mask
            * lax.psum_scatter(
                jnp.dot(
                    time_kernel.T,
                    operate_mixed.T,
                    precision=lax.Precision.HIGHEST,
                    preferred_element_type=jnp.float32,
                ),
                "tm",
                scatter_dimension=0,
                tiled=True,
            ).T
            + noise[:, None] * direction
        )
        curv = lax.psum(jnp.sum(direction * image), ("cfg", "tm"))
        alpha = norm_now / curv
        solution_field = solution_field + alpha * direction
        residual = residual - alpha * image
        norm_next = lax.psum(jnp.sum(residual * residual), ("cfg", "tm"))
        direction = residual + norm_next / norm_now * direction
        norm_now = norm_next
    return (solution_field, residual)


def solution(mesh):
    return jax.shard_map(
        body,
        mesh=mesh,
        in_specs=(P("cfg", "tm"), P("cfg", None), P(), P("cfg"), P("tm", None), P("cfg", "tm")),
        out_specs=(P("cfg", "tm"), P("cfg", "tm")),
        check_vma=False,
    )
```

profile of v0, /device:TPU:1, one launch (start us, length us, event | category | flops | bytes accessed | tf_op | source)
XLA Modules:
  0.0 509.3 jit_solution(8296447586257143950)
XLA Ops:
  7.2 0.0 copy-start
  7.2 0.0 all-gather.4.cloned.1.call-start
  7.2 1.6 multiply_reduce_fusion.5
  8.8 0.0 all-gather.4.cloned.1.call-update
  8.8 0.0 all-gather.6.cloned.1.call-start
  8.9 0.7 convert_element_type.5
  9.6 1.7 multiply_multiply_fusion
  11.2 0.0 all-gather.6.cloned.1.call-update
  11.3 0.0 reduce-scatter.3.cloned.1.call-start
  11.3 53.5 %all-gather.4.cloned.1.call-done = f32[8192,64]{0,1:T(8,128)} async-done(((f32[256,64]{0,1:T(8,128)}), f32[8192,64]{0,1:T(8,128)}) %all-gather.4.cloned.1.call-update) | async-done | bytes 2097168 | tf_op jit(solution)/shard_map/all_gather | solution.py:26
  64.8 1.8 multiply_reduce_fusion
  66.6 14.5 %exponential_multiply_fusion = f32[256,8192]{1,0:T(8,128)} fusion(f32[256,64]{0,1:T(8,128)} %get-tuple-element.7, f32[8192,64]{0,1:T(8,128)} %all-gather.4.cloned.1.call-done, f32[8192]{0:T(1024)S(1)} %multiply_reduce_fusion, f32[256]{0:T(256)S(1)} %get-tuple-element.6), kind=kOutput, calls=%fused_computation.5 | convolution fusion | flops 1627389952 | bytes 10585088 | tf_op jit(solution)/shard_map/dot_general | solution.py:11
  81.0 0.0 copy-start.1
  81.0 0.0 copy-start.3
  81.0 37.4 %all-gather.6.cloned.1.call-done = f32[8192,128]{1,0:T(8,128)} async-done(((f32[256,128]{1,0:T(8,128)}), f32[8192,128]{1,0:T(8,128)}) %all-gather.6.cloned.1.call-update) | async-done | bytes 4194320 | tf_op jit(solution)/shard_map/all_gather | solution.py:35
  118.5 9.8 %fusion.4 = f32[256,128]{1,0:T(8,128)S(1)} fusion(f32[256,8192]{1,0:T(8,128)} %exponential_multiply_fusion, f32[8192,128]{1,0:T(8,128)} %all-gather.6.cloned.1.call-done), kind=kOutput, calls=%fused_computation.23 | convolution fusion | flops 3221225472 | bytes 12713984 | tf_op jit(solution)/shard_map/dot_general | solution.py:33
  128.3 0.0 copy-done
  128.3 2.0 convolution_bitcast_fusion.1
  130.3 0.0 reduce-scatter.3.cloned.1.call-update
  130.4 0.0 all-gather.8.cloned.1.call-start
  130.4 33.7 %reduce-scatter.3.cloned.1.call-done = f32[128,256]{0,1:T(8,128)} async-done(((f32[1024,256]{0,1:T(8,128)}), f32[128,256]{0,1:T(8,128)}) %reduce-scatter.3.cloned.1.call-update) | async-done | bytes 131088 | tf_op jit(solution)/shard_map/reduce_scatter | solution.py:41
  164.1 0.0 copy-done.1
  164.1 0.0 copy-done.3
  164.1 0.0 copy-start.2
  164.1 1.8 multiply_reduce_fusion.3
  165.8 79.3 %all-reduce = (f32[]{:T(128)}, f32[]{:T(128)}) all-reduce(f32[]{:T(128)} %get-tuple-element.3, f32[]{:T(128)} %get-tuple-element.2), channel_id=1, replica_groups=mesh['cfg'=32,'tm'=8] {'cfg','tm'}, use_global_device_ids=true, to_apply=%region_1.0 | all-reduce | flops 2 | bytes 16 | tf_op jit(solution)/shard_map/psum | solution.py:31
  246.5 1.7 multiply_reduce_fusion.2
  248.2 73.5 %psum.30 = f32[]{:T(128)} all-reduce(f32[]{:T(128)} %multiply_reduce_fusion.2), channel_id=1, replica_groups=mesh['cfg'=32,'tm'=8] {'cfg','tm'}, use_global_device_ids=true, to_apply=%region_8.0 | all-reduce | flops 1 | bytes 8 | tf_op jit(solution)/shard_map/psum | solution.py:58
  323.0 1.7 broadcast_multiply_fusion
  324.8 0.0 all-gather.8.cloned.1.call-update
  324.8 0.0 reduce-scatter.5.cloned.1.call-start
  324.9 48.3 %all-gather.8.cloned.1.call-done = f32[8192,128]{1,0:T(8,128)} async-done(((f32[256,128]{1,0:T(8,128)}), f32[8192,128]{1,0:T(8,128)}) %all-gather.8.cloned.1.call-update) | async-done | bytes 4194320 | tf_op jit(solution)/shard_map/all_gather | solution.py:35
  373.2 9.8 %fusion.5 = f32[256,128]{1,0:T(8,128)S(1)} fusion(f32[256,8192]{1,0:T(8,128)} %exponential_multiply_fusion, f32[8192,128]{1,0:T(8,128)} %all-gather.8.cloned.1.call-done), kind=kOutput, calls=%fused_computation.24 | convolution fusion | flops 3221225472 | bytes 12713984 | tf_op jit(solution)/shard_map/dot_general | solution.py:33
  383.0 2.0 convolution_bitcast_fusion
  384.9 0.0 reduce-scatter.5.cloned.1.call-update
  385.0 33.1 %reduce-scatter.5.cloned.1.call-done = f32[128,256]{0,1:T(8,128)} async-done(((f32[1024,256]{0,1:T(8,128)}), f32[128,256]{0,1:T(8,128)}) %reduce-scatter.5.cloned.1.call-update) | async-done | bytes 131088 | tf_op jit(solution)/shard_map/reduce_scatter | solution.py:41
  418.1 0.0 copy-done.2
  418.1 1.7 multiply_reduce_fusion.1
  419.7 79.9 %psum.31 = f32[]{:T(128)} all-reduce(f32[]{:T(128)} %multiply_reduce_fusion.1), channel_id=1, replica_groups=mesh['cfg'=32,'tm'=8] {'cfg','tm'}, use_global_device_ids=true, to_apply=%region_11.0 | all-reduce | flops 1 | bytes 8 | tf_op jit(solution)/shard_map/psum | solution.py:54
  501.0 1.8 multiply_subtract_fusion
Async XLA Ops:
  7.2 121.1 %copy-start = (f32[128,1024]{1,0:T(8,128)S(1)}, f32[128,1024]{1,0:T(8,128)}, u32[]{:S(2)}) copy-start(f32[128,1024]{1,0:T(8,128)} %param.10) | copy-start | bytes 1572868
  7.2 57.6 %all-gather.4.cloned.1.call-start = ((), (), s32[]{:S(2)}) async-start(), calls=%async_computation.2 | async-start | bytes 2162688 | tf_op jit(solution)/shard_map/all_gather | solution.py:26
  8.8 109.6 %all-gather.6.cloned.1.call-start = ((), (), s32[]{:S(2)}) async-start(), calls=%async_computation.3 | async-start | bytes 4325376 | tf_op jit(solution)/shard_map/all_gather | solution.py:35
  11.3 152.8 %reduce-scatter.3.cloned.1.call-start = ((), (), s32[]{:S(2)}) async-start(), calls=%async_computation.4 | async-start | bytes 1179648 | tf_op jit(solution)/shard_map/reduce_scatter | solution.py:41
  81.0 83.0 %copy-start.1 = (f32[256,128]{1,0:T(8,128)S(1)}, f32[256,128]{1,0:T(8,128)}, u32[]{:S(2)}) copy-start(f32[256,128]{1,0:T(8,128)} %param.6) | copy-start | bytes 393220
  81.0 83.0 %copy-start.3 = (f32[256]{0:T(256)S(1)}, f32[256]{0:T(256)}, u32[]{:S(2)}) copy-start(f32[256]{0:T(256)} %param.9) | copy-start | bytes 3076
  130.4 242.8 %all-gather.8.cloned.1.call-start = ((), (), s32[]{:S(2)}) async-start(), calls=%async_computation.5 | async-start | bytes 4325376 | tf_op jit(solution)/shard_map/all_gather | solution.py:35
  164.1 254.0 %copy-start.2 = (f32[128,256]{0,1:T(8,128)S(1)}, f32[128,256]{0,1:T(8,128)}, u32[]{:S(2)}) copy-start(f32[128,256]{0,1:T(8,128)} %reduce-scatter.3.cloned.1.call-done) | copy-start | bytes 393220
  324.8 93.2 %reduce-scatter.5.cloned.1.call-start = ((), (), s32[]{:S(2)}) async-start(), calls=%async_computation.6 | async-start | bytes 1179648 | tf_op jit(solution)/shard_map/reduce_scatter | solution.py:41
Sparse Core Ops, SparseCore 0:
  11.0 53.7 all-gather.3
  67.9 50.5 all-gather.5
  130.5 33.5 reduce-scatter.2
  324.9 48.1 all-gather.7
  385.1 32.9 reduce-scatter.4
where the time goes:
time: 510 us; the launch traced here: 509 us
  blocking collectives  233 us (46%)
  waiting for transfers between devices  206 us (40%)
  matrix products  38.1 us (7%)
  between operations  17.8 us (3%)
  other arithmetic  14.4 us (3%)
    all_gather x2, waiting for transfers between devices, body(): lax.all_gather(mask * direction, 'cfg', axis=0, tiled=True)  85.7 us
    psum x1, blocking collectives, body(): curv = lax.psum(jnp.sum(direction * image), ('cfg', 'tm'))  79.9 us
    psum x1, blocking collectives, body(): norm_now = lax.psum(jnp.sum(residual * residual), ('cfg', 'tm'))  79.3 us
    psum x1, blocking collectives, body(): norm_next = lax.psum(jnp.sum(residual * residual), ('cfg', 'tm'))  73.5 us
    reduce_scatter x2, waiting for transfers between devices, body(): lax.psum_scatter(jnp.dot(time_kernel.T, operate_mixed.T, precision=lax.Pr...  66.7 us
    all_gather x1, waiting for transfers between devices, body(): every = lax.all_gather(scaled, 'cfg', axis=0, tiled=True)  53.5 us
    dot_general x2, matrix products, body(): jnp.dot(tile, lax.all_gather(mask * direction, 'cfg', axis=0, tiled=True)...  19.6 us
    dot_general x1, matrix products, matern(): jnp.dot(left, right.T, precision=lax.Precision.HIGHEST, preferred_element...  14.5 us
  transfers between devices with their start and end apart: 5, of which 5 were waited for; matrix products, arithmetic and copies ran while one was open for 4% of the time, Pallas kernels for 0%

commit v1 on v0

--- a/solution.py
+++ b/solution.py
@@ -5,6 +5,11 @@
 
 BLOCK = 128
 ITERS = 2
+
+
+def all_by_exchange(block, mesh_axis, d):
+    repeated = jnp.stack([block] * lax.axis_size(mesh_axis))
+    return jnp.concatenate(lax.all_to_all(repeated, mesh_axis, 0, 0), axis=d)
 
 
 def matern(left, right):
@@ -23,7 +28,7 @@
 def body(targets, features, inv_scales, noise, time_kernel, block_mask):
     mask = jnp.repeat(block_mask.astype(jnp.float32), BLOCK, axis=1)
     scaled = features * inv_scales[None, :]
-    every = lax.all_gather(scaled, "cfg", axis=0, tiled=True)
+    every = all_by_exchange(scaled, "cfg", 0)
     tile = matern(scaled, every)
     residual = mask * targets
     direction = residual

time: 510 us -> 468 us (0.918)
  waiting for transfers between devices: 206 us -> 128 us
  blocking collectives: 233 us -> 271 us
    all_gather x1 -> x0, waiting for transfers between devices: 53.5 us -> none  [body(): every = lax.all_gather(scaled, 'cfg', axis=0, tiled=True)]
    all_to_all x0 -> x1, blocking collectives: none -> 38.8 us  [all_by_exchange(): return jnp.concatenate(lax.all_to_all(repeated, mesh_axis, 0, 0), axis=d)]
    all_gather x2, waiting for transfers between devices: 85.7 us -> 61.1 us  [body(): lax.all_gather(mask * direction, 'cfg', axis=0, tiled=True)]
  transfers between devices with their start and end apart: 5 -> 4, of which waited for: 5 -> 4; matrix products, arithmetic and copies ran while one was open for 4% -> 3% of each run, Pallas kernels for 0% -> 0%
where the time goes in v1:
time: 468 us; the launch traced here: 467 us
  blocking collectives  271 us (58%)
  waiting for transfers between devices  128 us (27%)
  matrix products  36.8 us (8%)
  between operations  17.8 us (4%)
  other arithmetic  12.2 us (3%)
    psum x1, blocking collectives, body(): curv = lax.psum(jnp.sum(direction * image), ('cfg', 'tm'))  79.7 us
    psum x1, blocking collectives, body(): norm_now = lax.psum(jnp.sum(residual * residual), ('cfg', 'tm'))  79.5 us
    psum x1, blocking collectives, body(): norm_next = lax.psum(jnp.sum(residual * residual), ('cfg', 'tm'))  73.2 us
    reduce_scatter x2, waiting for transfers between devices, body(): lax.psum_scatter(jnp.dot(time_kernel.T, operate_mixed.T, precision=lax.Pr...  67 us
    all_gather x2, waiting for transfers between devices, body(): lax.all_gather(mask * direction, 'cfg', axis=0, tiled=True)  61.1 us
    all_to_all x1, blocking collectives, all_by_exchange(): return jnp.concatenate(lax.all_to_all(repeated, mesh_axis, 0, 0), axis=d)  38.8 us
    dot_general x2, matrix products, body(): jnp.dot(tile, lax.all_gather(mask * direction, 'cfg', axis=0, tiled=True)...  19.6 us
    dot_general x1, matrix products, matern(): jnp.dot(left, right.T, precision=lax.Precision.HIGHEST, preferred_element...  13.2 us
  transfers between devices with their start and end apart: 4, of which 4 were waited for; matrix products, arithmetic and copies ran while one was open for 3% of the time, Pallas kernels for 0%

profile of v1, /device:TPU:1, one launch (start us, length us, event | category | flops | bytes accessed | tf_op | source)
XLA Modules:
  0.0 466.8 jit_solution(6898170031612358138)
XLA Ops:
  7.2 0.0 copy-start
  7.2 0.0 all-gather.3.cloned.1.call-start
  7.2 0.7 convert_element_type.5
  8.0 1.7 multiply_multiply_fusion
  9.6 0.0 all-gather.3.cloned.1.call-update
  9.6 0.0 reduce-scatter.3.cloned.1.call-start
  9.7 0.9 multiply_reduce_fusion.5
  10.6 0.2 stack.2
  10.9 38.8 %all_to_all.5 = f32[32,256,64]{1,2,0:T(8,128)S(1)} all-to-all(f32[32,256,64]{1,2,0:T(8,128)S(1)} %stack.2), channel_id=1, replica_groups=mesh['cfg'=32,'tm'=8] {'cfg'}, dimensions={0} | all-to-all | bytes 4194304 | tf_op jit(solution)/shard_map/all_to_all | solution.py:12
  49.6 0.2 copy.10
  49.8 0.2 multiply_reduce_fusion
  50.1 13.2 %exponential_multiply_fusion = f32[256,8192]{1,0:T(8,128)} fusion(f32[256,64]{0,1:T(8,128)S(1)} %get-tuple-element.7, f32[8192,64]{0,1:T(8,128)S(1)} %bitcast.42, f32[8192]{0:T(1024)S(1)} %bitcast.50, f32[256]{0:T(256)S(1)} %get-tuple-element.6), kind=kOutput, calls=%fused_computation.5 | convolution fusion | flops 1627389952 | bytes 10585088 | tf_op jit(solution)/shard_map/dot_general | solution.py:16
  63.3 0.0 copy-start.1
  63.3 0.0 copy-start.3
  63.3 12.7 %all-gather.3.cloned.1.call-done = f32[8192,128]{1,0:T(8,128)} async-done(((f32[256,128]{1,0:T(8,128)}), f32[8192,128]{1,0:T(8,128)}) %all-gather.3.cloned.1.call-update) | async-done | bytes 4194320 | tf_op jit(solution)/shard_map/all_gather | solution.py:40
  76.0 9.8 %fusion.4 = f32[256,128]{1,0:T(8,128)S(1)} fusion(f32[256,8192]{1,0:T(8,128)} %exponential_multiply_fusion, f32[8192,128]{1,0:T(8,128)} %all-gather.3.cloned.1.call-done), kind=kOutput, calls=%fused_computation.23 | convolution fusion | flops 3221225472 | bytes 12713984 | tf_op jit(solution)/shard_map/dot_general | solution.py:38
  85.8 0.0 copy-done
  85.8 2.0 convolution_bitcast_fusion.1
  87.9 0.0 reduce-scatter.3.cloned.1.call-update
  87.9 0.0 all-gather.5.cloned.1.call-start
  87.9 33.8 %reduce-scatter.3.cloned.1.call-done = f32[128,256]{0,1:T(8,128)} async-done(((f32[1024,256]{0,1:T(8,128)}), f32[128,256]{0,1:T(8,128)}) %reduce-scatter.3.cloned.1.call-update) | async-done | bytes 131088 | tf_op jit(solution)/shard_map/reduce_scatter | solution.py:46
  121.7 0.0 copy-done.1
  121.7 0.0 copy-done.3
  121.7 0.0 copy-start.2
  121.7 1.8 multiply_reduce_fusion.3
  123.5 79.5 %all-reduce = (f32[]{:T(128)}, f32[]{:T(128)}) all-reduce(f32[]{:T(128)} %get-tuple-element.3, f32[]{:T(128)} %get-tuple-element.2), channel_id=1, replica_groups=mesh['cfg'=32,'tm'=8] {'cfg','tm'}, use_global_device_ids=true, to_apply=%region_1.0 | all-reduce | flops 2 | bytes 16 | tf_op jit(solution)/shard_map/psum | solution.py:36
  204.3 1.7 multiply_reduce_fusion.2
  206.0 73.2 %psum.30 = f32[]{:T(128)} all-reduce(f32[]{:T(128)} %multiply_reduce_fusion.2), channel_id=1, replica_groups=mesh['cfg'=32,'tm'=8] {'cfg','tm'}, use_global_device_ids=true, to_apply=%region_8.0 | all-reduce | flops 1 | bytes 8 | tf_op jit(solution)/shard_map/psum | solution.py:63
  280.5 1.7 broadcast_multiply_fusion
  282.3 0.0 all-gather.5.cloned.1.call-update
  282.3 0.0 reduce-scatter.5.cloned.1.call-start
  282.3 48.4 %all-gather.5.cloned.1.call-done = f32[8192,128]{1,0:T(8,128)} async-done(((f32[256,128]{1,0:T(8,128)}), f32[8192,128]{1,0:T(8,128)}) %all-gather.5.cloned.1.call-update) | async-done | bytes 4194320 | tf_op jit(solution)/shard_map/all_gather | solution.py:40
  330.7 9.8 %fusion.5 = f32[256,128]{1,0:T(8,128)S(1)} fusion(f32[256,8192]{1,0:T(8,128)} %exponential_multiply_fusion, f32[8192,128]{1,0:T(8,128)} %all-gather.5.cloned.1.call-done), kind=kOutput, calls=%fused_computation.24 | convolution fusion | flops 3221225472 | bytes 12713984 | tf_op jit(solution)/shard_map/dot_general | solution.py:38
  340.5 2.0 convolution_bitcast_fusion
  342.5 0.0 reduce-scatter.5.cloned.1.call-update
  342.5 33.3 %reduce-scatter.5.cloned.1.call-done = f32[128,256]{0,1:T(8,128)} async-done(((f32[1024,256]{0,1:T(8,128)}), f32[128,256]{0,1:T(8,128)}) %reduce-scatter.5.cloned.1.call-update) | async-done | bytes 131088 | tf_op jit(solution)/shard_map/reduce_scatter | solution.py:46
  375.8 0.0 copy-done.2
  375.8 1.7 multiply_reduce_fusion.1
  377.5 79.7 %psum.31 = f32[]{:T(128)} all-reduce(f32[]{:T(128)} %multiply_reduce_fusion.1), channel_id=1, replica_groups=mesh['cfg'=32,'tm'=8] {'cfg','tm'}, use_global_device_ids=true, to_apply=%region_11.0 | all-reduce | flops 1 | bytes 8 | tf_op jit(solution)/shard_map/psum | solution.py:59
  458.5 1.8 multiply_subtract_fusion
  (1 shorter events, 0.0 us)
Async XLA Ops:
  7.2 78.6 %copy-start = (f32[128,1024]{1,0:T(8,128)S(1)}, f32[128,1024]{1,0:T(8,128)}, u32[]{:S(2)}) copy-start(f32[128,1024]{1,0:T(8,128)} %param.10) | copy-start | bytes 1572868
  7.2 68.8 %all-gather.3.cloned.1.call-start = ((), (), s32[]{:S(2)}) async-start(), calls=%async_computation.3 | async-start | bytes 4325376 | tf_op jit(solution)/shard_map/all_gather | solution.py:40
  9.6 112.1 %reduce-scatter.3.cloned.1.call-start = ((), (), s32[]{:S(2)}) async-start(), calls=%async_computation.4 | async-start | bytes 1179648 | tf_op jit(solution)/shard_map/reduce_scatter | solution.py:46
  63.3 58.4 %copy-start.1 = (f32[256,128]{1,0:T(8,128)S(1)}, f32[256,128]{1,0:T(8,128)}, u32[]{:S(2)}) copy-start(f32[256,128]{1,0:T(8,128)} %param.6) | copy-start | bytes 393220
  63.3 58.4 %copy-start.3 = (f32[256]{0:T(256)S(1)}, f32[256]{0:T(256)}, u32[]{:S(2)}) copy-start(f32[256]{0:T(256)} %param.9) | copy-start | bytes 3076
  87.9 242.8 %all-gather.5.cloned.1.call-start = ((), (), s32[]{:S(2)}) async-start(), calls=%async_computation.5 | async-start | bytes 4325376 | tf_op jit(solution)/shard_map/all_gather | solution.py:40
  121.7 254.1 %copy-start.2 = (f32[128,256]{0,1:T(8,128)S(1)}, f32[128,256]{0,1:T(8,128)}, u32[]{:S(2)}) copy-start(f32[128,256]{0,1:T(8,128)} %reduce-scatter.3.cloned.1.call-done) | copy-start | bytes 393220
  282.3 93.5 %reduce-scatter.5.cloned.1.call-start = ((), (), s32[]{:S(2)}) async-start(), calls=%async_computation.6 | async-start | bytes 1179648 | tf_op jit(solution)/shard_map/reduce_scatter | solution.py:46
Sparse Core Ops, SparseCore 0:
  11.1 64.8 all-gather.2
  88.0 33.6 reduce-scatter.2
  282.4 48.2 all-gather.4
  342.6 33.1 reduce-scatter.4
